TPU v7x, 256 devices: a whole 4x4x8 slice. The times are simulated.
256 devices in a mesh: seq: 64 (over x, z_hi, y), dp: 4 (over z_lo, core).
Axes of the slice: x: 4, y: 4, z: 8 (z_hi: 4, z_lo: 2; z = z_hi * 2 + z_lo), core: 2. Of those that a mesh axis runs over, the one named last changes fastest.
Arguments:
- tokens: bfloat16 [32768, 1024], P(('dp', 'seq')), parts along dimension 0, may hold values from -6 to 6
- norm_gain: float32 [1024], replicated, may hold values from 0.1 to 1.9
- filters: float32 [12, 8192], P(None, 'seq'), may hold values from -0.0625 to 0.0625
- mixing: bfloat16 [12, 1024, 1024], P(None, 'seq'), may hold values from -0.0546875 to 0.0546875
Outputs:
- mixed: bfloat16 [32768, 1024], P(('dp', 'seq')), parts along dimension 0
There are 4 independent parts, one for each index of `dp`. A program takes and returns all parts, laid end to end along the dimension named above; an argument that names none is the same for every part. Nothing has to cross between parts.
All inputs are finite; a program needn't handle non-finite values.
Results may differ from a plain program's by a relative error of at most 0.0044.
Values may be sent and summed in bfloat16 or wider, within the bound.
A program may use at most 192 MiB of HBM per device.

v0:
```python
import math
import jax
import jax.numpy as jnp
from jax import lax
from jax.sharding import PartitionSpec as P

radix = 128
highest = lax.Precision.HIGHEST


def cos_sin(rows, cols, total):
    left = lax.broadcasted_iota(jnp.int32, (rows, cols), 0)
    right = lax.broadcasted_iota(jnp.int32, (rows, cols), 1)
    angle = (left * right % total).astype(jnp.float32) * (2.0 * math.pi / total)
    return (jnp.cos(angle), jnp.sin(angle))


def make_tables(blocks):
    total = blocks * radix
    half = blocks // 2
    cos_outer, sin_outer = cos_sin(blocks, half, blocks)
    cos_twid, sin_twid = cos_sin(blocks, radix, total)
    cos_inner, sin_inner = cos_sin(radix, radix, radix)
    cos_back, sin_back = cos_sin(half, blocks, blocks)
    return (
        cos_outer,
        sin_outer,
        cos_twid,
        sin_twid,
        cos_inner,
        sin_inner,
        cos_back,
        sin_back,
        total,
    )


def forward(signal, tables):
    cos_outer, sin_outer, cos_twid, sin_twid, cos_inner, sin_inner, cos_back, sin_back, total = (
        tables
    )
    first_re = jnp.einsum("kn,cna->cka", cos_outer, signal, precision=highest)
    first_im = -jnp.einsum("kn,cna->cka", sin_outer, signal, precision=highest)
    twist_re = first_re * cos_twid + first_im * sin_twid
    twist_im = first_im * cos_twid - first_re * sin_twid
    out_re = jnp.einsum("cka,aj->ckj", twist_re, cos_inner, precision=highest) + jnp.einsum(
        "cka,aj->ckj", twist_im, sin_inner, precision=highest
    )
    out_im = jnp.einsum("cka,aj->ckj", twist_im, cos_inner, precision=highest) - jnp.einsum(
        "cka,aj->ckj", twist_re, sin_inner, precision=highest
    )
    return (out_re, out_im)


def inverse(spec_re, spec_im, tables):
    cos_outer, sin_outer, cos_twid, sin_twid, cos_inner, sin_inner, cos_back, sin_back, total = (
        tables
    )
    inner_re = jnp.einsum("ckj,aj->cka", spec_re, cos_inner, precision=highest) - jnp.einsum(
        "ckj,aj->cka", spec_im, sin_inner, precision=highest
    )
    inner_im = jnp.einsum("ckj,aj->cka", spec_im, cos_inner, precision=highest) + jnp.einsum(
        "ckj,aj->cka", spec_re, sin_inner, precision=highest
    )
    twist_re = inner_re * cos_twid - inner_im * sin_twid
    twist_im = inner_im * cos_twid + inner_re * sin_twid
    result = jnp.einsum("nk,cka->cna", cos_back, twist_re, precision=highest) - jnp.einsum(
        "nk,cka->cna", sin_back, twist_im, precision=highest
    )
    return result / total


def local(tokens, norm_gain, filters, mixing):
    tok_rows, width = tokens.shape
    groups = lax.axis_size("seq")
    values = tokens.astype(jnp.float32)
    scale_row = lax.rsqrt(jnp.mean(values * values, axis=1, keepdims=True) + 1e-05)
    normed = (values * scale_row * norm_gain).astype(jnp.bfloat16)
    taps = lax.all_gather(filters, "seq", axis=1, tiled=True)
    num_filters, length = taps.shape
    blocks = 2 * length // radix
    half = blocks // 2
    tables = make_tables(blocks)
    phi_re, phi_im = forward(taps.reshape(num_filters, half, radix), tables)
    grouped = normed.reshape(tok_rows, groups, width // groups)
    piece = lax.all_to_all(grouped, "seq", split_axis=1, concat_axis=0, tiled=True)
    count = piece.shape[2]
    signal = piece[:, 0, :].astype(jnp.float32).T.reshape(count, half, radix)
    sig_re, sig_im = forward(signal, tables)

    def per_filter(spectrum):
        filt_re, filt_im = spectrum
        prod_re = sig_re * filt_re - sig_im * filt_im
        prod_im = sig_re * filt_im + sig_im * filt_re
        return inverse(prod_re, prod_im, tables).reshape(count, length).astype(jnp.bfloat16)

    features = lax.map(per_filter, (phi_re, phi_im))
    back = lax.all_to_all(features, "seq", split_axis=2, concat_axis=1, tiled=True)
    branch = jnp.einsum(
        "kct,kcd->td",
        back,
        lax.all_gather(mixing, "seq", axis=1, tiled=True),
        preferred_element_type=jnp.float32,
    )
    return (values + branch).astype(jnp.bfloat16)


def solution(mesh):
    in_specs = (P(("dp", "seq"), None), P(), P(None, "seq"), P(None, "seq", None))
    out_specs = P(("dp", "seq"), None)
    return jax.shard_map(local, mesh=mesh, in_specs=in_specs, out_specs=out_specs, check_vma=False)
```

profile of v0, /device:TPU:32, one launch (start us, length us, event | category | flops | bytes accessed | tf_op | source)
XLA Modules:
  0.0 559.1 jit_solution(12533361922189063383)
XLA Ops:
  10.3 13.7 %all-to-all-start = ((bf16[128,64,16]{0,2,1:T(8,128)(2,1)}), bf16[128,64,16]{0,2,1:T(8,128)(2,1)S(1)}, u32[]{:S(2)}, u32[]{:S(2)}) async-start(bf16[128,64,16]{0,2,1:T(8,128)(2,1)} %bitcast.6), calls=%async_computation | async-start | bytes 524288 | tf_op jit(solution)/shard_map/all_to_all | solution.py:86
  24.4 222.2 %all_gather.6 = f32[12,8192]{1,0:T(8,128)S(1)} all-gather(f32[12,128]{1,0:T(8,128)} %param.8), channel_id=1, replica_groups=mesh['seq'=64,'dp'=4] {'seq'}, dimensions={1}, use_global_device_ids=true | all-gather | bytes 399360 | tf_op jit(solution)/shard_map/all_gather | solution.py:79
  251.8 1.9 convolution_add_fusion.2
  255.5 2.0 fusion.102
  257.5 2.2 fusion.103
  259.7 2.0 convolution_add_fusion.1
  261.7 2.0 convolution_subtract_fusion.2
  263.7 106.2 %while.12 = (s32[]{:T(128)}, bf16[12,16,8192]{2,1,0:T(8,128)(2,1)}, f32[12,128,128]{2,1,0:T(8,128)}, f32[16,128,128]{2,1,0:T(8,128)S(1)}, f32[12,128,128]{2,1,0:...) while((s32[]{:T(128)}, bf16[12,16,8192]{2,1,0:T(8,128)(2,1)}, ...), condition=%wide.region_2.3_spmd.clone.clone, body=%wide.region_1.2_spmd.clone.clone.sunk | while | flops 2020278272 | bytes 22413904 | solution.py:97
  264.6 1.2 fusion.225
  282.3 1.2 fusion.225
  293.6 1.2 fusion.224
  320.2 1.2 fusion.224
  326.5 1.2 fusion.225
  329.0 1.2 fusion.224
  344.2 1.2 fusion.225
  353.1 1.2 fusion.225
  355.6 1.2 fusion.224
  361.9 1.2 fusion.225
  369.9 27.1 %copy.39 = bf16[12,16,8192]{1,0,2:T(8,128)(2,1)} copy(bf16[12,16,8192]{2,1,0:T(8,128)(2,1)} %get-tuple-element.79) | data formatting | bytes 6291456 | tf_op jit(solution)/shard_map/while | solution.py:97
  397.0 34.7 %reshape.71 = bf16[64,2,12288]{2,1,0:T(2,128)(2,1)S(1)} reshape(bf16[8192,12,16]{2,1,0:T(8,128)(2,1)} %bitcast.116) | data formatting | bytes 6291456
  431.7 46.9 %all_to_all.33 = bf16[64,2,12288]{2,1,0:T(2,128)(2,1)} all-to-all(bf16[64,2,12288]{2,1,0:T(2,128)(2,1)S(1)} %reshape.71), channel_id=1, replica_groups=mesh['seq'=64,'dp'=4] {'seq'}, dimensions={0} | all-to-all | bytes 6291456 | tf_op jit(solution)/shard_map/all_to_all | solution.py:98
  478.6 34.0 %reshape.72 = bf16[8192,12,16]{2,1,0:T(8,128)(2,1)} reshape(bf16[64,2,12288]{2,1,0:T(2,128)(2,1)} %all_to_all.33) | data formatting | bytes 6291456
  512.6 28.9 %copy.41 = bf16[12,64,16,128]{3,2,1,0:T(8,128)(2,1)S(1)} copy(bf16[12,64,16,128]{2,0,3,1:T(8,128)(2,1)} %bitcast.117) | data formatting | bytes 6291456 | tf_op jit(solution)/shard_map/all_to_all | solution.py:98
  541.5 10.7 %fusion.89 = bf16[128,1024]{1,0:T(8,128)(2,1)} fusion(bf16[12,1024,128]{2,1,0:T(8,128)(2,1)S(1)} %bitcast.118, bf16[12,1024,1024]{2,1,0:T(8,128)(2,1)} %all-gather.2.cloned.1.call-done, bf16[128,1024]{1,0:T(8,128)(2,1)S(1)} %copy-done), kind=kOutput, calls=%fused_computation.102 | convolution fusion | flops 3221618688 | bytes 28835840 | tf_op jit(solution)/shard_map/kct,kcd->td/dot_general | solution.py:99
  (135 shorter events, 104.1 us)
Async XLA Ops:
  6.5 535.0 %all-gather.2.cloned.1.call-start = ((), (), s32[]{:S(2)}) async-start(), calls=%async_computation.2 | async-start | bytes 25559040 | tf_op jit(solution)/shard_map/all_gather | solution.py:102
  10.3 243.4 %all-to-all-start = ((bf16[128,64,16]{0,2,1:T(8,128)(2,1)}), bf16[128,64,16]{0,2,1:T(8,128)(2,1)S(1)}, u32[]{:S(2)}, u32[]{:S(2)}) async-start(bf16[128,64,16]{0,2,1:T(8,128)(2,1)} %bitcast.6), calls=%async_computation | async-start | bytes 524288 | tf_op jit(solution)/shard_map/all_to_all | solution.py:86
  512.6 28.9 %copy-start = (bf16[128,1024]{1,0:T(8,128)(2,1)S(1)}, bf16[128,1024]{1,0:T(8,128)(2,1)}, u32[]{:S(2)}) copy-start(bf16[128,1024]{1,0:T(8,128)(2,1)} %param.6) | copy-start | bytes 786436
Sparse Core Ops, SparseCore 0:
  10.7 238.2 all-gather.1
where the time goes:
time: 563 us; the launch traced here: 559 us
  blocking collectives  269 us (48%)
  local copies, waits for them, and re-layouts  146 us (26%)
  matrix products  109 us (19%)
  starting transfers between devices  13.7 us (2%)
  between operations  13.6 us (2%)
  other arithmetic  5.77 us (1%)
    all_gather x1, blocking collectives, local(): taps = lax.all_gather(filters, 'seq', axis=1, tiled=True)  222 us
    unnamed x7, local copies, waits for them, and re-layouts  69 us
    all_to_all x1, blocking collectives, local(): lax.all_to_all(features, 'seq', split_axis=2, concat_axis=1, tiled=True)  46.9 us
    all_to_all x1, local copies, waits for them, and re-layouts, local(): lax.all_to_all(features, 'seq', split_axis=2, concat_axis=1, tiled=True)  28.9 us
    while x1, local copies, waits for them, and re-layouts, local(): features = lax.map(per_filter, (phi_re, phi_im))  27.1 us
    dot_general x12, matrix products, inverse(): jnp.einsum('ckj,aj->cka', spec_im, cos_inner, precision=highest)  14.9 us
    dot_general x12, matrix products, inverse(): jnp.einsum('ckj,aj->cka', spec_re, cos_inner, precision=highest)  14.9 us
    dot_general x12, matrix products, inverse(): jnp.einsum('ckj,aj->cka', spec_im, sin_inner, precision=highest)  14.8 us
  transfers between devices with their start and end apart: 2, of which 0 were waited for; matrix products, arithmetic and copies ran while one was open for 45% of the time, Pallas kernels for 0%

commit v1 on v0

--- a/solution.py
+++ b/solution.py
@@ -95,7 +95,10 @@
         return inverse(prod_re, prod_im, tables).reshape(count, length).astype(jnp.bfloat16)
 
     features = lax.map(per_filter, (phi_re, phi_im))
-    back = lax.all_to_all(features, "seq", split_axis=2, concat_axis=1, tiled=True)
+    back = jnp.concatenate(
+        lax.all_to_all(jnp.stack(jnp.split(features, lax.axis_size("seq"), axis=2)), "seq", 0, 0),
+        axis=1,
+    )
     branch = jnp.einsum(
         "kct,kcd->td",
         back,

time: 563 us -> 473 us (0.84)
  local copies, waits for them, and re-layouts: 146 us -> 49.4 us
  blocking collectives: 269 us -> 278 us
    unnamed x7 -> x70, local copies, waits for them, and re-layouts: 69 us -> 27.2 us
    all_to_all x1, local copies, waits for them, and re-layouts: 28.9 us -> 0.73 us  [local(): lax.all_to_all(jnp.stack(jnp.split(features, lax.axis_size('seq'), axis=2...]
    while x1 -> x0, local copies, waits for them, and re-layouts: 27.1 us -> none  [local(): features = lax.map(per_filter, (phi_re, phi_im))]
    all_to_all x1, blocking collectives: 46.9 us -> 64.6 us  [local(): lax.all_to_all(jnp.stack(jnp.split(features, lax.axis_size('seq'), axis=2...]
    all_gather x1, blocking collectives: 222 us -> 213 us  [local(): taps = lax.all_gather(filters, 'seq', axis=1, tiled=True)]
  transfers between devices with their start and end apart: 2 -> 2, of which waited for: 0 -> 0; matrix products, arithmetic and copies ran while one was open for 45% -> 32% of each run, Pallas kernels for 0% -> 0%
where the time goes in v1:
time: 473 us; the launch traced here: 471 us
  blocking collectives  278 us (59%)
  matrix products  109 us (23%)
  local copies, waits for them, and re-layouts  49.4 us (10%)
  starting transfers between devices  13.7 us (3%)
  between operations  13.7 us (3%)
  other arithmetic  5.77 us (1%)
    all_gather x1, blocking collectives, local(): taps = lax.all_gather(filters, 'seq', axis=1, tiled=True)  213 us
    all_to_all x1, blocking collectives, local(): lax.all_to_all(jnp.stack(jnp.split(features, lax.axis_size('seq'), axis=2...  64.6 us
    unnamed x70, local copies, waits for them, and re-layouts  27.2 us
    dot_general x12, matrix products, inverse(): jnp.einsum('ckj,aj->cka', spec_im, cos_inner, precision=highest)  14.9 us
    dot_general x12, matrix products, inverse(): jnp.einsum('ckj,aj->cka', spec_im, sin_inner, precision=highest)  14.9 us
    dot_general x12, matrix products, inverse(): jnp.einsum('ckj,aj->cka', spec_re, sin_inner, precision=highest)  14.8 us
    dot_general x12, matrix products, inverse(): jnp.einsum('ckj,aj->cka', spec_re, cos_inner, precision=highest)  14.8 us
    all_to_all x1, starting transfers between devices, local(): lax.all_to_all(grouped, 'seq', split_axis=1, concat_axis=0, tiled=True)  13.7 us
  transfers between devices with their start and end apart: 2, of which 0 were waited for; matrix products, arithmetic and copies ran while one was open for 32% of the time, Pallas kernels for 0%

profile of v1, /device:TPU:32, one launch (start us, length us, event | category | flops | bytes accessed | tf_op | source)
XLA Modules:
  0.0 470.8 jit_solution(14988345715707751712)
XLA Ops:
  9.6 13.7 %all-to-all-start = ((bf16[128,64,16]{0,2,1:T(8,128)(2,1)}), bf16[128,64,16]{0,2,1:T(8,128)(2,1)S(1)}, u32[]{:S(2)}, u32[]{:S(2)}) async-start(bf16[128,64,16]{0,2,1:T(8,128)(2,1)} %bitcast.6), calls=%async_computation | async-start | bytes 524288 | tf_op jit(solution)/shard_map/all_to_all | solution.py:86
  24.3 212.9 %all_gather.6 = f32[12,8192]{1,0:T(8,128)S(1)} all-gather(f32[12,128]{1,0:T(8,128)} %param.8), channel_id=1, replica_groups=mesh['seq'=64,'dp'=4] {'seq'}, dimensions={1}, use_global_device_ids=true | all-gather | bytes 399360 | tf_op jit(solution)/shard_map/all_gather | solution.py:79
  242.5 1.9 convolution_add_fusion.2
  246.2 2.0 fusion.102
  248.2 2.2 fusion.103
  250.4 2.0 convolution_add_fusion.1
  252.4 2.0 convolution_subtract_fusion.2
  254.4 106.3 %while.12 = (s32[]{:T(128)}, bf16[12,16,8192]{2,1,0:T(8,128)(2,1)}, f32[12,128,128]{2,1,0:T(8,128)}, f32[16,128,128]{2,1,0:T(8,128)S(1)}, f32[12,128,128]{2,1,0:...) while((s32[]{:T(128)}, bf16[12,16,8192]{2,1,0:T(8,128)(2,1)}, ...), condition=%wide.region_2.3_spmd.clone.clone, body=%wide.region_1.2_spmd.clone.clone.sunk | while | flops 2020278272 | bytes 22413904 | solution.py:97
  265.4 1.2 convolution_subtract_fusion.5
  266.7 1.2 fusion.224
  281.9 1.2 fusion.225
  284.4 1.2 fusion.224
  299.6 1.2 fusion.225
  302.1 1.2 fusion.224
  311.0 1.2 fusion.224
  319.8 1.2 fusion.224
  328.7 1.2 fusion.224
  335.0 1.2 fusion.225
  337.5 1.2 fusion.224
  346.4 1.2 fusion.224
  352.7 1.2 fusion.225
  355.2 1.2 fusion.224
  387.6 64.6 %all_to_all.20 = bf16[64,12,16,128]{3,2,1,0:T(8,128)(2,1)S(1)} all-to-all(bf16[64,12,16,128]{3,2,1,0:T(8,128)(2,1)S(1)} %constant_dynamic-update-slice_fusion.1), channel_id=1, replica_groups=mesh['seq'=64,'dp'=4] {'seq'}, dimensions={0} | all-to-all | bytes 6291456 | tf_op jit(solution)/shard_map/all_to_all | solution.py:99
  453.2 10.7 %fusion.89 = bf16[128,1024]{1,0:T(8,128)(2,1)} fusion(bf16[12,1024,128]{2,1,0:T(8,128)(2,1)S(1)} %bitcast.240, bf16[12,1024,1024]{2,1,0:T(8,128)(2,1)} %all-gather.2.cloned.1.call-done, bf16[128,1024]{1,0:T(8,128)(2,1)S(1)} %copy-done.1), kind=kOutput, calls=%fused_computation.102 | convolution fusion | flops 3221618688 | bytes 28835840 | tf_op jit(solution)/shard_map/kct,kcd->td/dot_general | solution.py:102
  (198 shorter events, 126.9 us)
Async XLA Ops:
  9.6 234.9 %all-to-all-start = ((bf16[128,64,16]{0,2,1:T(8,128)(2,1)}), bf16[128,64,16]{0,2,1:T(8,128)(2,1)S(1)}, u32[]{:S(2)}, u32[]{:S(2)}) async-start(bf16[128,64,16]{0,2,1:T(8,128)(2,1)} %bitcast.6), calls=%async_computation | async-start | bytes 524288 | tf_op jit(solution)/shard_map/all_to_all | solution.py:86
  23.2 429.8 %all-gather.2.cloned.1.call-start = ((), (), s32[]{:S(2)}) async-start(), calls=%async_computation.2 | async-start | bytes 25559040 | tf_op jit(solution)/shard_map/all_gather | solution.py:105
  360.8 26.0 %copy-start = (bf16[12,16,8192]{2,1,0:T(8,128)(2,1)S(1)}, bf16[12,16,8192]{2,1,0:T(8,128)(2,1)}, u32[]{:S(2)}) copy-start(bf16[12,16,8192]{2,1,0:T(8,128)(2,1)} %get-tuple-element.79) | copy-start | bytes 9437188
  452.2 1.0 copy-start.1
Sparse Core Ops, SparseCore 0:
  27.4 239.3 all-gather.1

commit v2 on v0

--- a/solution.py
+++ b/solution.py
@@ -76,7 +76,9 @@
     values = tokens.astype(jnp.float32)
     scale_row = lax.rsqrt(jnp.mean(values * values, axis=1, keepdims=True) + 1e-05)
     normed = (values * scale_row * norm_gain).astype(jnp.bfloat16)
-    taps = lax.all_gather(filters, "seq", axis=1, tiled=True)
+    taps = jnp.concatenate(
+        lax.all_to_all(jnp.stack([filters] * lax.axis_size("seq")), "seq", 0, 0), axis=1
+    )
     num_filters, length = taps.shape
     blocks = 2 * length // radix
     half = blocks // 2

time: 563 us -> 406 us (0.72)
  blocking collectives: 269 us -> 71.3 us
  waiting for transfers between devices: 0.73 us -> 34.5 us
    all_gather x1 -> x0, blocking collectives: 222 us -> none  [local(): taps = lax.all_gather(filters, 'seq', axis=1, tiled=True)]
    all_to_all x1, blocking collectives: 46.9 us -> 71.3 us  [local(): lax.all_to_all(features, 'seq', split_axis=2, concat_axis=1, tiled=True)]
    all_to_all x0 -> x1, waiting for transfers between devices: none -> 17 us  [local(): lax.all_to_all(jnp.stack([filters] * lax.axis_size('seq')), 'seq', 0, 0)]
    all_to_all x1, waiting for transfers between devices: 0.01 us -> 16.8 us  [local(): lax.all_to_all(grouped, 'seq', split_axis=1, concat_axis=0, tiled=True)]
    unnamed x7 -> x6, local copies, waits for them, and re-layouts: 69 us -> 69 us
  transfers between devices with their start and end apart: 2 -> 3, of which waited for: 0 -> 2; matrix products, arithmetic and copies ran while one was open for 45% -> 63% of each run, Pallas kernels for 0% -> 0%
where the time goes in v2:
time: 406 us; the launch traced here: 402 us
  local copies, waits for them, and re-layouts  148 us (36%)
  matrix products  109 us (27%)
  blocking collectives  71.3 us (18%)
  waiting for transfers between devices  34.5 us (8%)
  starting transfers between devices  19.2 us (5%)
  between operations  13.6 us (3%)
  other arithmetic  5.77 us (1%)
    all_to_all x1, blocking collectives, local(): lax.all_to_all(features, 'seq', split_axis=2, concat_axis=1, tiled=True)  71.3 us
    unnamed x6, local copies, waits for them, and re-layouts  69 us
    all_to_all x1, local copies, waits for them, and re-layouts, local(): lax.all_to_all(features, 'seq', split_axis=2, concat_axis=1, tiled=True)  28.9 us
    while x1, local copies, waits for them, and re-layouts, local(): features = lax.map(per_filter, (phi_re, phi_im))  27.1 us
    all_to_all x1, waiting for transfers between devices, local(): lax.all_to_all(jnp.stack([filters] * lax.axis_size('seq')), 'seq', 0, 0)  17 us
    all_to_all x1, waiting for transfers between devices, local(): lax.all_to_all(grouped, 'seq', split_axis=1, concat_axis=0, tiled=True)  16.8 us
    dot_general x12, matrix products, inverse(): jnp.einsum('ckj,aj->cka', spec_im, cos_inner, precision=highest)  14.9 us
    dot_general x12, matrix products, inverse(): jnp.einsum('ckj,aj->cka', spec_im, sin_inner, precision=highest)  14.9 us
  transfers between devices with their start and end apart: 3, of which 2 were waited for; matrix products, arithmetic and copies ran while one was open for 63% of the time, Pallas kernels for 0%

profile of v2, /device:TPU:32, one launch (start us, length us, event | category | flops | bytes accessed | tf_op | source)
XLA Modules:
  0.0 402.2 jit_solution(4407237507564421534)
XLA Ops:
  10.3 13.7 %all-to-all-start.1 = ((bf16[128,64,16]{0,2,1:T(8,128)(2,1)}), bf16[128,64,16]{0,2,1:T(8,128)(2,1)S(1)}, u32[]{:S(2)}, u32[]{:S(2)}) async-start(bf16[128,64,16]{0,2,1:T(8,128)(2,1)} %bitcast.7), calls=%async_computation.1 | async-start | bytes 524288 | tf_op jit(solution)/shard_map/all_to_all | solution.py:88
  24.4 16.8 %all-to-all-done.1 = bf16[128,64,16]{0,2,1:T(8,128)(2,1)S(1)} async-done(((bf16[128,64,16]{0,2,1:T(8,128)(2,1)}), bf16[128,64,16]{0,2,1:T(8,128)(2,1)S(1)}, u32[]{:S(2)}, u32[]{:S(2)}) %all-to-all-start.1) | async-done | bytes 262176 | tf_op jit(solution)/shard_map/all_to_all | solution.py:88
  41.2 1.5 stack.2
  42.7 5.5 %all-to-all-start = ((f32[64,12,128]{2,1,0:T(8,128)}), f32[64,12,128]{2,1,0:T(8,128)S(1)}, u32[]{:S(2)}, u32[]{:S(2)}) async-start(f32[64,12,128]{2,1,0:T(8,128)} %stack.2), calls=%async_computation | async-start | bytes 1048576 | tf_op jit(solution)/shard_map/all_to_all | solution.py:80
  50.0 2.0 fusion.104
  52.1 2.0 fusion.105
  54.1 2.0 convolution_add_fusion.1
  56.1 2.0 convolution_subtract_fusion.2
  58.1 17.0 %all-to-all-done = f32[64,12,128]{2,1,0:T(8,128)S(1)} async-done(((f32[64,12,128]{2,1,0:T(8,128)}), f32[64,12,128]{2,1,0:T(8,128)S(1)}, u32[]{:S(2)}, u32[]{:S(2)}) %all-to-all-start) | async-done | bytes 393248 | tf_op jit(solution)/shard_map/all_to_all | solution.py:80
  77.0 1.2 fusion.90
  80.3 1.9 convolution_add_fusion.2
  82.2 106.2 %while.12 = (s32[]{:T(128)}, bf16[12,16,8192]{2,1,0:T(8,128)(2,1)}, f32[12,128,128]{2,1,0:T(8,128)}, f32[16,128,128]{2,1,0:T(8,128)S(1)}, f32[12,128,128]{2,1,0:...) while((s32[]{:T(128)}, bf16[12,16,8192]{2,1,0:T(8,128)(2,1)}, ...), condition=%wide.region_2.3_spmd.clone.clone, body=%wide.region_1.2_spmd.clone.clone.sunk | while | flops 2020278272 | bytes 22413904 | solution.py:99
  85.6 1.2 fusion.226
  92.0 1.2 fusion.227
  93.2 1.2 convolution_subtract_fusion.5
  94.4 1.2 fusion.226
  103.3 1.2 fusion.226
  138.7 1.2 fusion.226
  188.5 27.1 %copy.40 = bf16[12,16,8192]{1,0,2:T(8,128)(2,1)} copy(bf16[12,16,8192]{2,1,0:T(8,128)(2,1)} %get-tuple-element.79) | data formatting | bytes 6291456 | tf_op jit(solution)/shard_map/while | solution.py:99
  215.6 34.8 %reshape.73 = bf16[64,2,12288]{2,1,0:T(2,128)(2,1)S(1)} reshape(bf16[8192,12,16]{2,1,0:T(8,128)(2,1)} %bitcast.118) | data formatting | bytes 6291456
  250.4 71.3 %all_to_all.38 = bf16[64,2,12288]{2,1,0:T(2,128)(2,1)} all-to-all(bf16[64,2,12288]{2,1,0:T(2,128)(2,1)S(1)} %reshape.73), channel_id=1, replica_groups=mesh['seq'=64,'dp'=4] {'seq'}, dimensions={0} | all-to-all | bytes 6291456 | tf_op jit(solution)/shard_map/all_to_all | solution.py:100
  321.7 34.0 %reshape.74 = bf16[8192,12,16]{2,1,0:T(8,128)(2,1)} reshape(bf16[64,2,12288]{2,1,0:T(2,128)(2,1)} %all_to_all.38) | data formatting | bytes 6291456
  355.7 28.9 %copy.42 = bf16[12,64,16,128]{3,2,1,0:T(8,128)(2,1)S(1)} copy(bf16[12,64,16,128]{2,0,3,1:T(8,128)(2,1)} %bitcast.119) | data formatting | bytes 6291456 | tf_op jit(solution)/shard_map/all_to_all | solution.py:100
  384.6 10.7 %fusion.89 = bf16[128,1024]{1,0:T(8,128)(2,1)} fusion(bf16[12,1024,128]{2,1,0:T(8,128)(2,1)S(1)} %bitcast.120, bf16[12,1024,1024]{2,1,0:T(8,128)(2,1)} %all-gather.2.cloned.1.call-done, bf16[128,1024]{1,0:T(8,128)(2,1)S(1)} %copy-done), kind=kOutput, calls=%fused_computation.102 | convolution fusion | flops 3221618688 | bytes 28835840 | tf_op jit(solution)/shard_map/kct,kcd->td/dot_general | solution.py:101
  (136 shorter events, 108.0 us)
Async XLA Ops:
  6.5 378.1 %all-gather.2.cloned.1.call-start = ((), (), s32[]{:S(2)}) async-start(), calls=%async_computation.3 | async-start | bytes 25559040 | tf_op jit(solution)/shard_map/all_gather | solution.py:104
  10.3 30.9 %all-to-all-start.1 = ((bf16[128,64,16]{0,2,1:T(8,128)(2,1)}), bf16[128,64,16]{0,2,1:T(8,128)(2,1)S(1)}, u32[]{:S(2)}, u32[]{:S(2)}) async-start(bf16[128,64,16]{0,2,1:T(8,128)(2,1)} %bitcast.7), calls=%async_computation.1 | async-start | bytes 524288 | tf_op jit(solution)/shard_map/all_to_all | solution.py:88
  42.7 32.3 %all-to-all-start = ((f32[64,12,128]{2,1,0:T(8,128)}), f32[64,12,128]{2,1,0:T(8,128)S(1)}, u32[]{:S(2)}, u32[]{:S(2)}) async-start(f32[64,12,128]{2,1,0:T(8,128)} %stack.2), calls=%async_computation | async-start | bytes 1048576 | tf_op jit(solution)/shard_map/all_to_all | solution.py:80
  355.7 28.9 %copy-start = (bf16[128,1024]{1,0:T(8,128)(2,1)S(1)}, bf16[128,1024]{1,0:T(8,128)(2,1)}, u32[]{:S(2)}) copy-start(bf16[128,1024]{1,0:T(8,128)(2,1)} %param.6) | copy-start | bytes 786436
Sparse Core Ops, SparseCore 0:
  10.7 240.8 all-gather.1
